TPU v7x, 256 devices: a whole 4x4x8 slice. The times are simulated.
256 devices in a mesh: lat: 4 (over y_lo, core), lon: 64 (over z, x, y_hi).
Axes of the slice: x: 4, y: 4 (y_hi: 2, y_lo: 2; y = y_hi * 2 + y_lo), z: 8, core: 2. Of those that a mesh axis runs over, the one named last changes fastest.
Arguments:
- residual: bfloat16 [128, 1024, 128], P('lat', 'lon'), may hold values from -6 to 6
- noise_weights: float32 [128, 1024], P('lat', 'lon'), may hold values from 0.5 to 4
- kernel: bfloat16 [4, 1, 2048, 2048], P(None, None, 'lat'), may hold values from -0.0625 to 0.0625
Outputs:
- gradient: float32 [1, 128, 1024, 128], P(None, 'lat', 'lon')
All inputs are finite; a program needn't handle non-finite values.
Results may differ from a plain program's by a relative error of at most 0.0029.
Values may be sent and summed in bfloat16 or wider, within the bound.
No kernel may reach another device: no remote copies, remote signals or barrier semaphores. Data moves between devices by JAX's collectives and lax.ppermute only.
A program may use at most 64 MiB of HBM per device.

v0:
```python
import jax
import jax.numpy as jnp
from jax import lax
from jax.experimental import pallas as pl
from jax.experimental.pallas import tpu as pltpu
from jax.sharding import PartitionSpec as P


VMEM = pl.BlockSpec(memory_space=pltpu.VMEM)
HBM = pl.BlockSpec(memory_space=pltpu.HBM)


def in_hbm(value):
    return pltpu.with_memory_space_constraint(value, pltpu.HBM)


def eastward(value, by):
    length = lax.axis_size("lon")
    return lax.ppermute(value, "lon", [(i, (i + by) % length) for i in range(length)])


def swapped(value, mask):
    length = lax.axis_size("lat")
    return lax.ppermute(value, "lat", [(i, i ^ mask) for i in range(length)])


def eastward_swapped(value, by, mask):
    lats, lons = lax.axis_size("lat"), lax.axis_size("lon")
    pairs = [
        (b * lons + j, (b ^ mask) * lons + (j + by) % lons) for b in range(lats) for j in range(lons)
    ]
    return lax.ppermute(value, ("lat", "lon"), pairs)


def call(body, outs, in_specs, scratch, flops, nbytes, limit):
    return pl.pallas_call(
        body,
        out_shape=outs,
        in_specs=in_specs,
        out_specs=jax.tree.map(lambda _: VMEM, outs),
        scratch_shapes=scratch,
        cost_estimate=pl.CostEstimate(flops=flops, bytes_accessed=nbytes, transcendentals=0),
        compiler_params=pltpu.CompilerParams(vmem_limit_bytes=limit),
    )


def weighted_part(data, weights, first):
    part = [
        (weights[:, first + y : first + y + 1] * data[y].astype(jnp.float32)).astype(jnp.bfloat16)
        for y in range(data.shape[0])
    ]
    return jnp.concatenate(part, axis=0).T


def product(weighted, panel):
    return jnp.dot(weighted, panel, preferred_element_type=jnp.float32)


def bands(cells):
    band = lax.axis_index("lat")
    partner = band + 1 - 2 * (band % 2)
    order = (band, 3 - partner, partner, 3 - band)
    return [pl.ds(pl.multiple_of(b * cells, cells), cells) for b in order]


def early_body(residual, noise, panels, here, east, staged, data, weights, held, weighted, sems):
    pieces, rows = data.shape[0], data.shape[1]
    cells = rows * data.shape[2]
    copies = [pltpu.make_async_copy(noise, weights, sems.at[0])]
    for i in range(pieces):
        source = residual.at[pl.ds(i * rows, rows)]
        copies.append(pltpu.make_async_copy(source, data.at[i], sems.at[1 + i]))
    for d in range(4):
        target = held.at[d] if d < 2 else staged.at[d - 2]
        copies.append(pltpu.make_async_copy(panels.at[d, 0], target, sems.at[1 + pieces + d]))
    for copy in copies:
        copy.start()
    copies[0].wait()
    for i in range(pieces):
        copies[1 + i].wait()
        weighted[:, i * cells : (i + 1) * cells] = weighted_part(data.at[i], weights, i * rows)
    block = weighted.shape[1]
    for d, acc in ((0, here), (1, east)):
        copies[1 + pieces + d].wait()
        for k in range(panels.shape[3] // block):
            where = slice(k * block, (k + 1) * block)
            acc[:, where] = product(weighted[...], held[d, :, where])
    for d in (2, 3):
        copies[1 + pieces + d].wait()


def partner_east_body(data, weights, staged, east, weighted, out):
    weighted[...] = weighted_part(data, weights, 0)
    _, _, near, far = bands(weighted.shape[1])
    for i, where in enumerate((near, far)):
        total = east[:, where] + product(weighted[...], staged[1, :, where])
        out[i] = total.astype(out.dtype)


def rest_body(weighted, staged, here, east, away, mine):
    own, own_far, near, far = bands(weighted.shape[1])
    for i, where in enumerate((far, near)):
        total = here[:, where] + product(weighted[...], staged[0, :, where])
        away[i] = total.astype(away.dtype)
    for i, where in enumerate((own, own_far)):
        mine[i] = east[:, where] + product(weighted[...], staged[1, :, where])
    for i, where in enumerate((own, own_far)):
        mine[2 + i] = here[:, where] + product(weighted[...], staged[0, :, where])


def pack_east_body(mine, other, near, far):
    near[...] = (mine[0] + other[0].astype(jnp.float32)).astype(near.dtype)
    far[...] = (mine[1] + other[1].astype(jnp.float32)).astype(far.dtype)


def pack_here_body(mine, other, far):
    far[...] = (mine[3] + other[0].astype(jnp.float32)).astype(far.dtype)


def final_body(mine, other, r1, r2, r3, out):
    total = mine[2] + other[1].astype(jnp.float32)
    for r in (r1, r2, r3):
        total += r[...].astype(jnp.float32)
    out[...] = total.T


def sweep(residual, noise_weights, kernel):
    rows, columns, probes = residual.shape
    cells = rows * columns
    every = kernel.shape[3]
    f32, bf16 = jnp.float32, jnp.bfloat16
    shape = jax.ShapeDtypeStruct
    MB = 1 << 20
    pieces = 4
    noise = noise_weights.T

    data2 = eastward(residual, 2)
    noise2 = eastward(noise, 2)
    part = shape((probes, cells), bf16)
    flops = 2 * probes * cells * cells
    here, east, staged = call(
        early_body,
        (shape((probes, every), f32), shape((probes, every), f32), shape((2, cells, every), bf16)),
        [HBM] * 3,
        [
            pltpu.VMEM((pieces, rows // pieces, columns, probes), bf16),
            pltpu.VMEM((columns, rows), f32),
            pltpu.VMEM((2, cells, every), bf16),
            pltpu.VMEM((probes, cells), bf16),
            pltpu.SemaphoreType.DMA((pieces + 5,)),
        ],
        8 * flops,
        10 * MB,
        16 * MB,
    )(in_hbm(residual), in_hbm(noise), in_hbm(kernel))
    weighted2, away = call(
        partner_east_body, (part, shape((2, probes, cells), bf16)), [VMEM] * 4, [], 2 * flops, 2 * MB, 8 * MB
    )(data2, noise2, staged, east)
    other_east = swapped(away, 1)
    away, mine = call(
        rest_body,
        (shape((2, probes, cells), bf16), shape((4, probes, cells), f32)),
        [VMEM] * 4,
        [],
        6 * flops,
        6 * MB,
        8 * MB,
    )(weighted2, staged, here, east)
    other_here = swapped(away, 1)
    near, far = call(pack_east_body, (part, part), [VMEM] * 2, [], 0, MB, 4 * MB)(mine, other_east)
    r1 = eastward(near, 1)
    r2 = eastward_swapped(far, 1, 2)
    far = call(pack_here_body, part, [VMEM] * 2, [], 0, MB, 4 * MB)(mine, other_here)
    r3 = swapped(far, 2)
    total = call(final_body, shape((cells, probes), f32), [VMEM] * 5, [], 0, MB, 4 * MB)(
        mine, other_here, r3, r2, r1
    )
    return total.reshape(1, rows, columns, probes)


def solution(mesh):
    return jax.shard_map(
        sweep,
        mesh=mesh,
        in_specs=(P("lat", "lon", None), P("lat", "lon"), P(None, None, "lat", None)),
        out_specs=P(None, "lat", "lon", None),
        check_vma=False,
    )
```

profile of v0, /device:TPU:1, one launch (start us, length us, event | category | flops | bytes accessed | tf_op | source)
XLA Modules:
  0.0 30.3 jit_solution(16782452108928609521)
XLA Ops:
  0.0 2.0 %collective-permute-start = (bf16[32,16,128]{2,1,0:T(8,128)(2,1)}, bf16[32,16,128]{2,1,0:T(8,128)(2,1)S(1)}, u32[]{:S(2)}, u32[]{:S(2)}) collective-permute-start(bf16[32,16,128]{2,1,0:T(8,128)(2,1)} %residual.1), channel_id=1, source_target_pairs={{0,2},{1,3},{2,4},{3,5},{4,6},{5,7},{6,8},{7,9},{8,10},{9,11},{10,... | collective-permute-start | bytes 393224 | tf_op jit(solution)/shard_map/ppermute | solution.py:19
  2.0 1.2 %collective-permute-start.1 = (f32[16,32]{1,0:T(8,128)}, f32[16,32]{1,0:T(8,128)S(1)}, u32[]{:S(2)}, u32[]{:S(2)}) collective-permute-start(f32[16,32]{1,0:T(8,128)} %bitcast.2), channel_id=1, source_target_pairs={{0,2},{1,3},{2,4},{3,5},{4,6},{5,7},{6,8},{7,9},{8,10},{9,11},{10,... | collective-permute-start | bytes 6152 | tf_op jit(solution)/shard_map/ppermute | solution.py:19
  3.2 3.6 %shard_map.37 = (f32[128,2048]{1,0:T(8,128)S(1)}, f32[128,2048]{1,0:T(8,128)S(1)}, bf16[2,512,2048]{2,1,0:T(8,128)(2,1)S(1)}) custom-call(bf16[32,16,128]{2,1,0:T(8,128)(2,1)} %residual.1, f32[16,32]{1,0:T(8,128)} %bitcast.3, bf16[4,1,512,2048]{3,2,1,0:T(8,128)(2,1)} %panels.1), custom_call_target="tpu_custom_call" | custom-call | flops 536870912 | bytes 10485760 | tf_op jit(solution)/shard_map/pallas_call | solution.py:141
  6.9 5.3 %collective-permute-done.1.weights = f32[16,32]{1,0:T(8,128)S(1)} collective-permute-done((f32[16,32]{1,0:T(8,128)}, f32[16,32]{1,0:T(8,128)S(1)}, u32[]{:S(2)}, u32[]{:S(2)}) %collective-permute-start.1) | collective-permute-done | bytes 2080 | tf_op jit(solution)/shard_map/ppermute | solution.py:19
  12.2 0.0 collective-permute-done.data
  12.2 0.5 %shard_map.38 = (bf16[128,512]{1,0:T(8,128)(2,1)S(1)}, bf16[2,128,512]{2,1,0:T(8,128)(2,1)S(1)}) custom-call(bf16[32,16,128]{2,1,0:T(8,128)(2,1)S(1)} %collective-permute-done.data, f32[16,32]{1,0:T(8,128)S(1)} %collective-permute-done.1.weights, bf16[2,512,2048]{2,1,0:T(8,128)(2,1)S(1)} %get-tuple-element.14.staged, f32[128,2048]{1,0:T(8,128)S(1)} %get-tuple-element.15.east), custom_call_target="tpu_custom_call" | custom-call | flops 134217728 | bytes 2097152 | tf_op jit(solution)/shard_map/pallas_call | solution.py:156
  12.6 0.6 %shard_map.39 = (bf16[2,128,512]{2,1,0:T(8,128)(2,1)S(1)}, f32[4,128,512]{2,1,0:T(8,128)S(1)}) custom-call(bf16[128,512]{1,0:T(8,128)(2,1)S(1)} %get-tuple-element.16.weighted, bf16[2,512,2048]{2,1,0:T(8,128)(2,1)S(1)} %get-tuple-element.14.staged, f32[128,2048]{1,0:T(8,128)S(1)} %get-tuple-element.17.here, f32[128,2048]{1,0:T(8,128)S(1)} %get-tuple-element.15.east), custom_call_target="tpu_custom_call" | custom-call | flops 402653184 | bytes 6291456 | tf_op jit(solution)/shard_map/pallas_call | solution.py:160
  13.3 1.3 %collective-permute-start.2 = (bf16[2,128,512]{2,1,0:T(8,128)(2,1)S(1)}, bf16[2,128,512]{2,1,0:T(8,128)(2,1)S(1)}, u32[]{:S(2)}, u32[]{:S(2)}) collective-permute-start(bf16[2,128,512]{2,1,0:T(8,128)(2,1)S(1)} %get-tuple-element.19), channel_id=1, source_target_pairs={{0,64},{64,0},{128,192},{192,128},{1,65},{65,1},{129,193},{193,129... | collective-permute-start | bytes 786440 | tf_op jit(solution)/shard_map/ppermute | solution.py:24
  14.6 0.1 collective-permute-start.4
  14.7 1.1 %collective-permute-done.2.other = bf16[2,128,512]{2,1,0:T(8,128)(2,1)S(1)} collective-permute-done((bf16[2,128,512]{2,1,0:T(8,128)(2,1)S(1)}, bf16[2,128,512]{2,1,0:T(8,128)(2,1)S(1)}, u32[]{:S(2)}, u32[]{:S(2)}) %collective-permute-start.2) | collective-permute-done | bytes 262176 | tf_op jit(solution)/shard_map/ppermute | solution.py:24
  15.8 1.4 %collective-permute-start.3 = (bf16[128,512]{1,0:T(8,128)(2,1)S(1)}, bf16[128,512]{1,0:T(8,128)(2,1)S(1)}, u32[]{:S(2)}, u32[]{:S(2)}) collective-permute-start(bf16[128,512]{1,0:T(8,128)(2,1)S(1)} %shard_map.40), channel_id=1, source_target_pairs={{0,128},{64,192},{128,0},{192,64},{1,129},{65,193},{129,1},{193,65... | collective-permute-start | bytes 393224 | tf_op jit(solution)/shard_map/ppermute | solution.py:24
  17.2 0.0 collective-permute-done.4.other
  17.2 2.0 %collective-permute-start.5 = (bf16[128,512]{1,0:T(8,128)(2,1)S(1)}, bf16[128,512]{1,0:T(8,128)(2,1)S(1)}, u32[]{:S(2)}, u32[]{:S(2)}) collective-permute-start(bf16[128,512]{1,0:T(8,128)(2,1)S(1)} %get-tuple-element.21), channel_id=1, source_target_pairs={{0,129},{1,130},{2,131},{3,132},{4,133},{5,134},{6,135},{7,136},{8... | collective-permute-start | bytes 393224 | tf_op jit(solution)/shard_map/ppermute | solution.py:32
  19.2 0.8 %collective-permute-start.6 = (bf16[128,512]{1,0:T(8,128)(2,1)S(1)}, bf16[128,512]{1,0:T(8,128)(2,1)S(1)}, u32[]{:S(2)}, u32[]{:S(2)}) collective-permute-start(bf16[128,512]{1,0:T(8,128)(2,1)S(1)} %get-tuple-element.22), channel_id=1, source_target_pairs={{0,1},{1,2},{2,3},{3,4},{4,5},{5,6},{6,7},{7,8},{8,9},{9,10},{10,1... | collective-permute-start | bytes 393224 | tf_op jit(solution)/shard_map/ppermute | solution.py:19
  20.0 0.5 %collective-permute-done.3.r1 = bf16[128,512]{1,0:T(8,128)(2,1)S(1)} collective-permute-done((bf16[128,512]{1,0:T(8,128)(2,1)S(1)}, bf16[128,512]{1,0:T(8,128)(2,1)S(1)}, u32[]{:S(2)}, u32[]{:S(2)}) %collective-permute-start.3) | collective-permute-done | bytes 131104 | tf_op jit(solution)/shard_map/ppermute | solution.py:24
  20.6 6.6 %collective-permute-done.5.r2 = bf16[128,512]{1,0:T(8,128)(2,1)S(1)} collective-permute-done((bf16[128,512]{1,0:T(8,128)(2,1)S(1)}, bf16[128,512]{1,0:T(8,128)(2,1)S(1)}, u32[]{:S(2)}, u32[]{:S(2)}) %collective-permute-start.5) | collective-permute-done | bytes 131104 | tf_op jit(solution)/shard_map/ppermute | solution.py:32
  27.1 2.3 %collective-permute-done.6.r3 = bf16[128,512]{1,0:T(8,128)(2,1)S(1)} collective-permute-done((bf16[128,512]{1,0:T(8,128)(2,1)S(1)}, bf16[128,512]{1,0:T(8,128)(2,1)S(1)}, u32[]{:S(2)}, u32[]{:S(2)}) %collective-permute-start.6) | collective-permute-done | bytes 131104 | tf_op jit(solution)/shard_map/ppermute | solution.py:19
  29.4 0.8 %shard_map.42 = f32[512,128]{1,0:T(8,128)} custom-call(f32[4,128,512]{2,1,0:T(8,128)S(1)} %get-tuple-element.18.mine, bf16[2,128,512]{2,1,0:T(8,128)(2,1)S(1)} %collective-permute-done.2.other, bf16[128,512]{1,0:T(8,128)(2,1)S(1)} %collective-permute-done.3.r1, bf16[128,512]{1,0:T(8,128)(2,1)S(1)} %collective-permute-done.5.r2, ...), custom_call_target="tpu_custom_call" | custom-call | bytes 1048576 | tf_op jit(solution)/shard_map/pallas_call | solution.py:175
  (2 shorter events, 0.1 us)
Async XLA Ops:
  0.0 12.2 %collective-permute-start = (bf16[32,16,128]{2,1,0:T(8,128)(2,1)}, bf16[32,16,128]{2,1,0:T(8,128)(2,1)S(1)}, u32[]{:S(2)}, u32[]{:S(2)}) collective-permute-start(bf16[32,16,128]{2,1,0:T(8,128)(2,1)} %residual.1), channel_id=1, source_target_pairs={{0,2},{1,3},{2,4},{3,5},{4,6},{5,7},{6,8},{7,9},{8,10},{9,11},{10,... | collective-permute-start | bytes 393224 | tf_op jit(solution)/shard_map/ppermute | solution.py:19
  2.0 10.1 %collective-permute-start.1 = (f32[16,32]{1,0:T(8,128)}, f32[16,32]{1,0:T(8,128)S(1)}, u32[]{:S(2)}, u32[]{:S(2)}) collective-permute-start(f32[16,32]{1,0:T(8,128)} %bitcast.2), channel_id=1, source_target_pairs={{0,2},{1,3},{2,4},{3,5},{4,6},{5,7},{6,8},{7,9},{8,10},{9,11},{10,... | collective-permute-start | bytes 6152 | tf_op jit(solution)/shard_map/ppermute | solution.py:19
  13.3 2.5 %collective-permute-start.2 = (bf16[2,128,512]{2,1,0:T(8,128)(2,1)S(1)}, bf16[2,128,512]{2,1,0:T(8,128)(2,1)S(1)}, u32[]{:S(2)}, u32[]{:S(2)}) collective-permute-start(bf16[2,128,512]{2,1,0:T(8,128)(2,1)S(1)} %get-tuple-element.19), channel_id=1, source_target_pairs={{0,64},{64,0},{128,192},{192,128},{1,65},{65,1},{129,193},{193,129... | collective-permute-start | bytes 786440 | tf_op jit(solution)/shard_map/ppermute | solution.py:24
  14.6 2.6 %collective-permute-start.4 = (bf16[2,128,512]{2,1,0:T(8,128)(2,1)S(1)}, bf16[2,128,512]{2,1,0:T(8,128)(2,1)S(1)}, u32[]{:S(2)}, u32[]{:S(2)}) collective-permute-start(bf16[2,128,512]{2,1,0:T(8,128)(2,1)S(1)} %get-tuple-element.20), channel_id=1, source_target_pairs={{0,64},{64,0},{128,192},{192,128},{1,65},{65,1},{129,193},{193,129... | collective-permute-start | bytes 786440 | tf_op jit(solution)/shard_map/ppermute | solution.py:24
  15.8 4.8 %collective-permute-start.3 = (bf16[128,512]{1,0:T(8,128)(2,1)S(1)}, bf16[128,512]{1,0:T(8,128)(2,1)S(1)}, u32[]{:S(2)}, u32[]{:S(2)}) collective-permute-start(bf16[128,512]{1,0:T(8,128)(2,1)S(1)} %shard_map.40), channel_id=1, source_target_pairs={{0,128},{64,192},{128,0},{192,64},{1,129},{65,193},{129,1},{193,65... | collective-permute-start | bytes 393224 | tf_op jit(solution)/shard_map/ppermute | solution.py:24
  17.2 9.9 %collective-permute-start.5 = (bf16[128,512]{1,0:T(8,128)(2,1)S(1)}, bf16[128,512]{1,0:T(8,128)(2,1)S(1)}, u32[]{:S(2)}, u32[]{:S(2)}) collective-permute-start(bf16[128,512]{1,0:T(8,128)(2,1)S(1)} %get-tuple-element.21), channel_id=1, source_target_pairs={{0,129},{1,130},{2,131},{3,132},{4,133},{5,134},{6,135},{7,136},{8... | collective-permute-start | bytes 393224 | tf_op jit(solution)/shard_map/ppermute | solution.py:32
  19.2 10.2 %collective-permute-start.6 = (bf16[128,512]{1,0:T(8,128)(2,1)S(1)}, bf16[128,512]{1,0:T(8,128)(2,1)S(1)}, u32[]{:S(2)}, u32[]{:S(2)}) collective-permute-start(bf16[128,512]{1,0:T(8,128)(2,1)S(1)} %get-tuple-element.22), channel_id=1, source_target_pairs={{0,1},{1,2},{2,3},{3,4},{4,5},{5,6},{6,7},{7,8},{8,9},{9,10},{10,1... | collective-permute-start | bytes 393224 | tf_op jit(solution)/shard_map/ppermute | solution.py:19
where the time goes:
time: 30.4 us; the launch traced here: 30.3 us
  waiting for transfers between devices  15.8 us (52%)
  starting transfers between devices  8.85 us (29%)
  Pallas kernels  5.61 us (18%)
    ppermute x3, waiting for transfers between devices, eastward(): lax.ppermute(value, 'lon', [(i, (i + by) % length) for i in range(length)])  7.62 us
    ppermute x1, waiting for transfers between devices, eastward_swapped(): return lax.ppermute(value, ('lat', 'lon'), pairs)  6.56 us
    ppermute x3, starting transfers between devices, eastward(): lax.ppermute(value, 'lon', [(i, (i + by) % length) for i in range(length)])  4.05 us
    pallas_call x1, Pallas kernels, sweep(): call(early_body, (shape((probes, every), f32), shape((probes, every), f32...  3.63 us
    ppermute x3, starting transfers between devices, swapped(): return lax.ppermute(value, 'lat', [(i, i ^ mask) for i in range(length)])  2.8 us
    ppermute x1, starting transfers between devices, eastward_swapped(): return lax.ppermute(value, ('lat', 'lon'), pairs)  2 us
    ppermute x3, waiting for transfers between devices, swapped(): return lax.ppermute(value, 'lat', [(i, i ^ mask) for i in range(length)])  1.6 us
    pallas_call x1, Pallas kernels, sweep(): call(final_body, shape((cells, probes), f32), [VMEM] * 5, [], 0, MB, 4 * MB)  0.84 us
  transfers between devices with their start and end apart: 7, of which 5 were waited for; matrix products, arithmetic and copies ran while one was open for 0% of the time, Pallas kernels for 12%

commit v1 on v0

v1 whole, which is shorter than its diff:
```python
import jax
import jax.numpy as jnp
from jax import lax
from jax.experimental import pallas as pl
from jax.experimental.pallas import tpu as pltpu
from jax.sharding import PartitionSpec as P


SEGMENT = 8

VMEM = pl.BlockSpec(memory_space=pltpu.VMEM)
HBM = pl.BlockSpec(memory_space=pltpu.HBM)


def in_hbm(value):
    return pltpu.with_memory_space_constraint(value, pltpu.HBM)


def lon_pairs(by, wanted):
    length = lax.axis_size("lon")
    return [((i - by) % length, i) for i in range(length) if wanted(i % SEGMENT == 0)]


def eastward(value, by, wanted=lambda first: True):
    return lax.ppermute(value, "lon", lon_pairs(by, wanted))


def swapped(value, mask):
    length = lax.axis_size("lat")
    return lax.ppermute(value, "lat", [(i, i ^ mask) for i in range(length)])


def eastward_swapped(value, by, mask, wanted):
    lats, lons = lax.axis_size("lat"), lax.axis_size("lon")
    pairs = [(b * lons + i, (b ^ mask) * lons + j) for b in range(lats) for i, j in lon_pairs(by, wanted)]
    return lax.ppermute(value, ("lat", "lon"), pairs)


def call(body, outs, in_specs, scratch, flops, nbytes, limit):
    return pl.pallas_call(
        body,
        out_shape=outs,
        in_specs=in_specs,
        out_specs=jax.tree.map(lambda _: VMEM, outs),
        scratch_shapes=scratch,
        cost_estimate=pl.CostEstimate(flops=flops, bytes_accessed=nbytes, transcendentals=0),
        compiler_params=pltpu.CompilerParams(vmem_limit_bytes=limit),
    )


def weigh_body(residual, noise, out, data, weights, sems):
    copies = [
        pltpu.make_async_copy(noise, weights, sems.at[0]),
        pltpu.make_async_copy(residual, data, sems.at[1]),
    ]
    for copy in copies:
        copy.start()
    for copy in copies:
        copy.wait()
    part = [
        (weights[:, y : y + 1] * data[y].astype(jnp.float32)).astype(out.dtype)
        for y in range(data.shape[0])
    ]
    out[...] = jnp.concatenate(part, axis=0).T


def product(weighted, panel):
    return jnp.dot(weighted, panel, preferred_element_type=jnp.float32)


def bands(cells):
    band = lax.axis_index("lat")
    partner = band + 1 - 2 * (band % 2)
    order = (band, 3 - partner, partner, 3 - band)
    return [pl.ds(pl.multiple_of(b * cells, cells), cells) for b in order]


def early_body(weighted, panels, here, east, staged, held, sems):
    copies = [pltpu.make_async_copy(panels.at[0, 0], held, sems.at[0])]
    for d in range(1, 4):
        copies.append(pltpu.make_async_copy(panels.at[d, 0], staged.at[d - 1], sems.at[d]))
    for copy in copies:
        copy.start()
    block = weighted.shape[1]
    for d, acc, panel in ((0, here, held), (1, east, staged.at[0])):
        copies[d].wait()
        for k in range(panels.shape[3] // block):
            where = slice(k * block, (k + 1) * block)
            acc[:, where] = product(weighted[...], panel[:, where])
    for copy in copies[2:]:
        copy.wait()


def partner_east_body(weighted, staged, east, out):
    _, _, near, far = bands(weighted.shape[1])
    for i, where in enumerate((near, far)):
        total = east[:, where] + product(weighted[...], staged[2, :, where])
        out[i] = total.astype(out.dtype)


def rest_body(weighted, w1, w3, staged, here, east, away, mine, total):
    own, own_far, near, far = bands(weighted.shape[1])
    for i, where in enumerate((own, own_far)):
        mine[i] = east[:, where] + product(weighted[...], staged[2, :, where])
    order = (own, own_far, far, near)
    for i, where in enumerate(order):
        total[i] = here[:, where] + product(weighted[...], staged[1, :, where])

    @pl.when(lax.axis_index("lon") % SEGMENT == 0)
    def _():
        for i, where in enumerate(order):
            total[i] += product(w1[...], staged[0, :, where]) + product(w3[...], staged[2, :, where])

    for i in range(2):
        mine[2 + i] = total[i]
        away[i] = total[2 + i].astype(away.dtype)


def pack_east_body(mine, other, near, far):
    near[...] = (mine[0] + other[0].astype(jnp.float32)).astype(near.dtype)
    far[...] = (mine[1] + other[1].astype(jnp.float32)).astype(far.dtype)


def pack_here_body(mine, other, far):
    far[...] = (mine[3] + other[0].astype(jnp.float32)).astype(far.dtype)


def final_body(mine, other, r1, r2, r3, out):
    total = mine[2] + other[1].astype(jnp.float32)
    for r in (r1, r2, r3):
        total += r[...].astype(jnp.float32)
    out[...] = total.T


def sweep(residual, noise_weights, kernel):
    rows, columns, probes = residual.shape
    cells = rows * columns
    every = kernel.shape[3]
    f32, bf16 = jnp.float32, jnp.bfloat16
    shape = jax.ShapeDtypeStruct
    MB = 1 << 20
    part = shape((probes, cells), bf16)
    flops = 2 * probes * cells * cells

    weighted = call(
        weigh_body,
        pltpu.VMEM((probes, cells), bf16),
        [HBM] * 2,
        [
            pltpu.VMEM((rows, columns, probes), bf16),
            pltpu.VMEM((columns, rows), f32),
            pltpu.SemaphoreType.DMA((2,)),
        ],
        0,
        MB // 4,
        4 * MB,
    )(in_hbm(residual), in_hbm(noise_weights.T))
    w2 = eastward(weighted, 2)
    w1 = eastward(weighted, 1, lambda first: first)
    w3 = eastward(weighted, 3, lambda first: first)
    here, east, staged = call(
        early_body,
        (shape((probes, every), f32), shape((probes, every), f32), shape((3, cells, every), bf16)),
        [VMEM, HBM],
        [pltpu.VMEM((cells, every), bf16), pltpu.SemaphoreType.DMA((4,))],
        8 * flops,
        10 * MB,
        16 * MB,
    )(weighted, in_hbm(kernel))
    away = call(partner_east_body, shape((2, probes, cells), bf16), [VMEM] * 3, [], 2 * flops, 2 * MB, 8 * MB)(
        w2, staged, east
    )
    other_east = swapped(away, 1)
    away, mine = call(
        rest_body,
        (shape((2, probes, cells), bf16), shape((4, probes, cells), f32)),
        [VMEM] * 6,
        [pltpu.VMEM((4, probes, cells), f32)],
        6 * flops,
        6 * MB,
        8 * MB,
    )(w2, w1, w3, staged, here, east)
    other_here = swapped(away, 1)
    near, far = call(pack_east_body, (part, part), [VMEM] * 2, [], 0, MB, 4 * MB)(mine, other_east)
    r1 = eastward(near, 1, lambda first: not first)
    r2 = eastward_swapped(far, 1, 2, lambda first: not first)
    far = call(pack_here_body, part, [VMEM] * 2, [], 0, MB, 4 * MB)(mine, other_here)
    r3 = swapped(far, 2)
    total = call(final_body, shape((cells, probes), f32), [VMEM] * 5, [], 0, MB, 4 * MB)(
        mine, other_here, r3, r2, r1
    )
    return total.reshape(1, rows, columns, probes)


def solution(mesh):
    return jax.shard_map(
        sweep,
        mesh=mesh,
        in_specs=(P("lat", "lon", None), P("lat", "lon"), P(None, None, "lat", None)),
        out_specs=P(None, "lat", "lon", None),
        check_vma=False,
    )
```

time: 30.4 us -> 36.1 us (1.19)
  the two profiles are of different devices: /device:TPU:1 before, /device:TPU:2 now
where the time goes in v1:
time: 36.1 us; the launch traced here: 36 us
  waiting for transfers between devices  15 us (42%)
  starting transfers between devices  14.3 us (40%)
  Pallas kernels  6.57 us (18%)
    ppermute x1, waiting for transfers between devices, eastward_swapped(): return lax.ppermute(value, ('lat', 'lon'), pairs)  10.2 us
    ppermute x1, starting transfers between devices, eastward_swapped(): return lax.ppermute(value, ('lat', 'lon'), pairs)  7.3 us
    ppermute x4, starting transfers between devices, eastward(): return lax.ppermute(value, 'lon', lon_pairs(by, wanted))  5.86 us
    ppermute x4, waiting for transfers between devices, eastward(): return lax.ppermute(value, 'lon', lon_pairs(by, wanted))  4.11 us
    pallas_call x1, Pallas kernels, sweep(): call(early_body, (shape((probes, every), f32), shape((probes, every), f32...  3.5 us
    pallas_call x1, Pallas kernels, sweep(): call(weigh_body, pltpu.VMEM((probes, cells), bf16), [HBM] * 2, [pltpu.VME...  1.16 us
    ppermute x3, starting transfers between devices, swapped(): return lax.ppermute(value, 'lat', [(i, i ^ mask) for i in range(length)])  1.15 us
    pallas_call x1, Pallas kernels, sweep(): call(final_body, shape((cells, probes), f32), [VMEM] * 5, [], 0, MB, 4 * MB)  0.84 us
  transfers between devices with their start and end apart: 8, of which 4 were waited for; matrix products, arithmetic and copies ran while one was open for 0% of the time, Pallas kernels for 11%

profile of v1, /device:TPU:2, one launch (start us, length us, event | category | flops | bytes accessed | tf_op | source)
XLA Modules:
  0.0 36.0 jit_solution(12142137716253431840)
XLA Ops:
  0.0 1.2 %shard_map.37.weighted = bf16[128,512]{1,0:T(8,128)(2,1)S(1)} custom-call(bf16[32,16,128]{2,1,0:T(8,128)(2,1)} %residual.1, f32[16,32]{1,0:T(8,128)} %bitcast.2), custom_call_target="tpu_custom_call" | custom-call | bytes 262144 | tf_op jit(solution)/shard_map/pallas_call | solution.py:145
  1.2 0.7 %collective-permute-start.2 = (bf16[128,512]{1,0:T(8,128)(2,1)S(1)}, bf16[128,512]{1,0:T(8,128)(2,1)S(1)}, u32[]{:S(2)}, u32[]{:S(2)}) collective-permute-start(bf16[128,512]{1,0:T(8,128)(2,1)S(1)} %shard_map.37.weighted), channel_id=1, source_target_pairs={{61,0},{5,8},{13,16},{21,24},{29,32},{37,40},{45,48},{53,56},{125,... | collective-permute-start | bytes 393224 | tf_op jit(solution)/shard_map/ppermute | solution.py:25
  1.8 0.7 %collective-permute-start.1 = (bf16[128,512]{1,0:T(8,128)(2,1)S(1)}, bf16[128,512]{1,0:T(8,128)(2,1)S(1)}, u32[]{:S(2)}, u32[]{:S(2)}) collective-permute-start(bf16[128,512]{1,0:T(8,128)(2,1)S(1)} %shard_map.37.weighted), channel_id=1, source_target_pairs={{63,0},{7,8},{15,16},{23,24},{31,32},{39,40},{47,48},{55,56},{127,... | collective-permute-start | bytes 393224 | tf_op jit(solution)/shard_map/ppermute | solution.py:25
  2.5 1.6 %collective-permute-start = (bf16[128,512]{1,0:T(8,128)(2,1)S(1)}, bf16[128,512]{1,0:T(8,128)(2,1)S(1)}, u32[]{:S(2)}, u32[]{:S(2)}) collective-permute-start(bf16[128,512]{1,0:T(8,128)(2,1)S(1)} %shard_map.37.weighted), channel_id=1, source_target_pairs={{62,0},{63,1},{0,2},{1,3},{2,4},{3,5},{4,6},{5,7},{6,8},{7,9},{8,1... | collective-permute-start | bytes 393224 | tf_op jit(solution)/shard_map/ppermute | solution.py:25
  4.1 3.5 %shard_map.38 = (f32[128,2048]{1,0:T(8,128)S(1)}, f32[128,2048]{1,0:T(8,128)S(1)}, bf16[3,512,2048]{2,1,0:T(8,128)(2,1)S(1)}) custom-call(bf16[128,512]{1,0:T(8,128)(2,1)S(1)} %shard_map.37.weighted, bf16[4,1,512,2048]{3,2,1,0:T(8,128)(2,1)} %panels.1), custom_call_target="tpu_custom_call" | custom-call | flops 536870912 | bytes 10485760 | tf_op jit(solution)/shard_map/pallas_call | solution.py:161
  7.6 0.0 collective-permute-done.2.w3
  7.6 0.0 collective-permute-done.1.w1
  7.6 1.4 %collective-permute-done.weighted = bf16[128,512]{1,0:T(8,128)(2,1)S(1)} collective-permute-done((bf16[128,512]{1,0:T(8,128)(2,1)S(1)}, bf16[128,512]{1,0:T(8,128)(2,1)S(1)}, u32[]{:S(2)}, u32[]{:S(2)}) %collective-permute-start) | collective-permute-done | bytes 131104 | tf_op jit(solution)/shard_map/ppermute | solution.py:25
  9.0 0.7 %shard_map.39 = (bf16[2,128,512]{2,1,0:T(8,128)(2,1)S(1)}, f32[4,128,512]{2,1,0:T(8,128)S(1)}) custom-call(bf16[128,512]{1,0:T(8,128)(2,1)S(1)} %collective-permute-done.weighted, bf16[128,512]{1,0:T(8,128)(2,1)S(1)} %collective-permute-done.1.w1, bf16[128,512]{1,0:T(8,128)(2,1)S(1)} %collective-permute-done.2.w3, ...), custom_call_target="tpu_custom_call" | custom-call | flops 402653184 | bytes 6291456 | tf_op jit(solution)/shard_map/pallas_call | solution.py:174
  9.7 0.1 collective-permute-start.3
  9.8 0.3 shard_map.41
  10.1 0.6 %collective-permute-start.5 = (bf16[2,128,512]{2,1,0:T(8,128)(2,1)S(1)}, bf16[2,128,512]{2,1,0:T(8,128)(2,1)S(1)}, u32[]{:S(2)}, u32[]{:S(2)}) collective-permute-start(bf16[2,128,512]{2,1,0:T(8,128)(2,1)S(1)} %shard_map.41), channel_id=1, source_target_pairs={{0,64},{64,0},{128,192},{192,128},{1,65},{65,1},{129,193},{193,129... | collective-permute-start | bytes 786440 | tf_op jit(solution)/shard_map/ppermute | solution.py:30
  10.7 0.6 %collective-permute-done.3.other = bf16[2,128,512]{2,1,0:T(8,128)(2,1)S(1)} collective-permute-done((bf16[2,128,512]{2,1,0:T(8,128)(2,1)S(1)}, bf16[2,128,512]{2,1,0:T(8,128)(2,1)S(1)}, u32[]{:S(2)}, u32[]{:S(2)}) %collective-permute-start.3) | collective-permute-done | bytes 262176 | tf_op jit(solution)/shard_map/ppermute | solution.py:30
  11.4 0.5 %collective-permute-start.4 = (bf16[128,512]{1,0:T(8,128)(2,1)S(1)}, bf16[128,512]{1,0:T(8,128)(2,1)S(1)}, u32[]{:S(2)}, u32[]{:S(2)}) collective-permute-start(bf16[128,512]{1,0:T(8,128)(2,1)S(1)} %shard_map.40), channel_id=1, source_target_pairs={{0,128},{64,192},{128,0},{192,64},{1,129},{65,193},{129,1},{193,65... | collective-permute-start | bytes 393224 | tf_op jit(solution)/shard_map/ppermute | solution.py:30
  11.9 0.0 collective-permute-done.5.other
  11.9 7.3 %collective-permute-start.6 = (bf16[128,512]{1,0:T(8,128)(2,1)S(1)}, bf16[128,512]{1,0:T(8,128)(2,1)S(1)}, u32[]{:S(2)}, u32[]{:S(2)}) collective-permute-start(bf16[128,512]{1,0:T(8,128)(2,1)S(1)} %get-tuple-element.17), channel_id=1, source_target_pairs={{0,129},{1,130},{2,131},{3,132},{4,133},{5,134},{6,135},{8,137},{9... | collective-permute-start | bytes 393224 | tf_op jit(solution)/shard_map/ppermute | solution.py:36
  19.2 3.0 %collective-permute-start.7 = (bf16[128,512]{1,0:T(8,128)(2,1)S(1)}, bf16[128,512]{1,0:T(8,128)(2,1)S(1)}, u32[]{:S(2)}, u32[]{:S(2)}) collective-permute-start(bf16[128,512]{1,0:T(8,128)(2,1)S(1)} %get-tuple-element.18), channel_id=1, source_target_pairs={{0,1},{1,2},{2,3},{3,4},{4,5},{5,6},{6,7},{8,9},{9,10},{10,11},{11... | collective-permute-start | bytes 393224 | tf_op jit(solution)/shard_map/ppermute | solution.py:25
  22.2 0.0 collective-permute-done.4.r1
  22.2 10.2 %collective-permute-done.6.r2 = bf16[128,512]{1,0:T(8,128)(2,1)S(1)} collective-permute-done((bf16[128,512]{1,0:T(8,128)(2,1)S(1)}, bf16[128,512]{1,0:T(8,128)(2,1)S(1)}, u32[]{:S(2)}, u32[]{:S(2)}) %collective-permute-start.6) | collective-permute-done | bytes 131104 | tf_op jit(solution)/shard_map/ppermute | solution.py:36
  32.4 2.7 %collective-permute-done.7.r3 = bf16[128,512]{1,0:T(8,128)(2,1)S(1)} collective-permute-done((bf16[128,512]{1,0:T(8,128)(2,1)S(1)}, bf16[128,512]{1,0:T(8,128)(2,1)S(1)}, u32[]{:S(2)}, u32[]{:S(2)}) %collective-permute-start.7) | collective-permute-done | bytes 131104 | tf_op jit(solution)/shard_map/ppermute | solution.py:25
  35.1 0.8 %shard_map.43 = f32[512,128]{1,0:T(8,128)} custom-call(f32[4,128,512]{2,1,0:T(8,128)S(1)} %get-tuple-element.15.mine, bf16[2,128,512]{2,1,0:T(8,128)(2,1)S(1)} %collective-permute-done.3.other, bf16[128,512]{1,0:T(8,128)(2,1)S(1)} %collective-permute-done.4.r1, bf16[128,512]{1,0:T(8,128)(2,1)S(1)} %collective-permute-done.6.r2, ...), custom_call_target="tpu_custom_call" | custom-call | bytes 1048576 | tf_op jit(solution)/shard_map/pallas_call | solution.py:189
  (2 shorter events, 0.1 us)
Async XLA Ops:
  1.2 6.4 %collective-permute-start.2 = (bf16[128,512]{1,0:T(8,128)(2,1)S(1)}, bf16[128,512]{1,0:T(8,128)(2,1)S(1)}, u32[]{:S(2)}, u32[]{:S(2)}) collective-permute-start(bf16[128,512]{1,0:T(8,128)(2,1)S(1)} %shard_map.37.weighted), channel_id=1, source_target_pairs={{61,0},{5,8},{13,16},{21,24},{29,32},{37,40},{45,48},{53,56},{125,... | collective-permute-start | bytes 393224 | tf_op jit(solution)/shard_map/ppermute | solution.py:25
  1.8 5.8 %collective-permute-start.1 = (bf16[128,512]{1,0:T(8,128)(2,1)S(1)}, bf16[128,512]{1,0:T(8,128)(2,1)S(1)}, u32[]{:S(2)}, u32[]{:S(2)}) collective-permute-start(bf16[128,512]{1,0:T(8,128)(2,1)S(1)} %shard_map.37.weighted), channel_id=1, source_target_pairs={{63,0},{7,8},{15,16},{23,24},{31,32},{39,40},{47,48},{55,56},{127,... | collective-permute-start | bytes 393224 | tf_op jit(solution)/shard_map/ppermute | solution.py:25
  2.5 6.5 %collective-permute-start = (bf16[128,512]{1,0:T(8,128)(2,1)S(1)}, bf16[128,512]{1,0:T(8,128)(2,1)S(1)}, u32[]{:S(2)}, u32[]{:S(2)}) collective-permute-start(bf16[128,512]{1,0:T(8,128)(2,1)S(1)} %shard_map.37.weighted), channel_id=1, source_target_pairs={{62,0},{63,1},{0,2},{1,3},{2,4},{3,5},{4,6},{5,7},{6,8},{7,9},{8,1... | collective-permute-start | bytes 393224 | tf_op jit(solution)/shard_map/ppermute | solution.py:25
  9.7 1.6 %collective-permute-start.3 = (bf16[2,128,512]{2,1,0:T(8,128)(2,1)S(1)}, bf16[2,128,512]{2,1,0:T(8,128)(2,1)S(1)}, u32[]{:S(2)}, u32[]{:S(2)}) collective-permute-start(bf16[2,128,512]{2,1,0:T(8,128)(2,1)S(1)} %get-tuple-element.16), channel_id=1, source_target_pairs={{0,64},{64,0},{128,192},{192,128},{1,65},{65,1},{129,193},{193,129... | collective-permute-start | bytes 786440 | tf_op jit(solution)/shard_map/ppermute | solution.py:30
  10.1 1.7 %collective-permute-start.5 = (bf16[2,128,512]{2,1,0:T(8,128)(2,1)S(1)}, bf16[2,128,512]{2,1,0:T(8,128)(2,1)S(1)}, u32[]{:S(2)}, u32[]{:S(2)}) collective-permute-start(bf16[2,128,512]{2,1,0:T(8,128)(2,1)S(1)} %shard_map.41), channel_id=1, source_target_pairs={{0,64},{64,0},{128,192},{192,128},{1,65},{65,1},{129,193},{193,129... | collective-permute-start | bytes 786440 | tf_op jit(solution)/shard_map/ppermute | solution.py:30
  11.4 10.8 %collective-permute-start.4 = (bf16[128,512]{1,0:T(8,128)(2,1)S(1)}, bf16[128,512]{1,0:T(8,128)(2,1)S(1)}, u32[]{:S(2)}, u32[]{:S(2)}) collective-permute-start(bf16[128,512]{1,0:T(8,128)(2,1)S(1)} %shard_map.40), channel_id=1, source_target_pairs={{0,128},{64,192},{128,0},{192,64},{1,129},{65,193},{129,1},{193,65... | collective-permute-start | bytes 393224 | tf_op jit(solution)/shard_map/ppermute | solution.py:30
  11.9 20.5 %collective-permute-start.6 = (bf16[128,512]{1,0:T(8,128)(2,1)S(1)}, bf16[128,512]{1,0:T(8,128)(2,1)S(1)}, u32[]{:S(2)}, u32[]{:S(2)}) collective-permute-start(bf16[128,512]{1,0:T(8,128)(2,1)S(1)} %get-tuple-element.17), channel_id=1, source_target_pairs={{0,129},{1,130},{2,131},{3,132},{4,133},{5,134},{6,135},{8,137},{9... | collective-permute-start | bytes 393224 | tf_op jit(solution)/shard_map/ppermute | solution.py:36
  19.2 15.9 %collective-permute-start.7 = (bf16[128,512]{1,0:T(8,128)(2,1)S(1)}, bf16[128,512]{1,0:T(8,128)(2,1)S(1)}, u32[]{:S(2)}, u32[]{:S(2)}) collective-permute-start(bf16[128,512]{1,0:T(8,128)(2,1)S(1)} %get-tuple-element.18), channel_id=1, source_target_pairs={{0,1},{1,2},{2,3},{3,4},{4,5},{5,6},{6,7},{8,9},{9,10},{10,11},{11... | collective-permute-start | bytes 393224 | tf_op jit(solution)/shard_map/ppermute | solution.py:25
